TPU v7x, 32 devices: a whole 2x2x4 slice. The times are simulated.
32 devices in a mesh: seq: 4 (over z), head: 8 (over y, x, core).
Axes of the slice: x: 2, y: 2, z: 4, core: 2. Of those that a mesh axis runs over, the one named last changes fastest.
Arguments:
- query: float32 [3072, 1024], P('seq', 'head'), may hold values from -6 to 6
- key_in: float32 [3072, 1024], P('seq', 'head'), may hold values from -6 to 6
- value: float32 [3072, 1024], P('seq', 'head'), may hold values from -6 to 6
- out_grad: float32 [3072, 1024], P('seq', 'head'), may hold values from -6 to 6
- head_scale: float32 [8], P('head'), may hold values from 0.5 to 2
- norm_gain: float32 [1024], P('head'), may hold values from 0.5 to 1.5
- group_counts: int32 [4], replicated, may hold values from 1 to 6, 12 in all
Outputs:
- normed: float32 [3072, 1024], P('seq', 'head')
- grad_query: float32 [3072, 1024], P('seq', 'head')
- grad_key: float32 [3072, 1024], P('seq', 'head')
- grad_value: float32 [3072, 1024], P('seq', 'head')
Inputs may be any that keep to these rules, and one draw needn't show every extreme that they name: The live rows of shard i are its first 128 * group_counts[i] rows; the counts sum to 3 * 4 and the largest is exactly 6.
All inputs are finite; a program needn't handle non-finite values.
Results may differ from a plain program's by a relative error of at most 0.0001.
Values sent between devices are 32-bit elements; how exact they have to be, the bound alone decides.
A program may use at most 64 MiB of HBM per device.

v0:
```python
import jax
import jax.numpy as jnp
from jax import lax
from jax.sharding import PartitionSpec as P

GROUP = 128


def plain_product(left, right):
    return jnp.dot(left, right, precision=lax.Precision.HIGHEST, preferred_element_type=jnp.float32)


def leading_product(left, right):
    return lax.dot_general(
        left,
        right,
        (((0,), (0,)), ((), ())),
        precision=lax.Precision.HIGHEST,
        preferred_element_type=jnp.float32,
    )


def on_device(query, key_in, value, out_grad, head_scale, norm_gain, group_counts):
    capacity, features_dev = query.shape
    shard_pos = lax.axis_index("seq")
    block_live = group_counts[shard_pos]
    live_rows = (jnp.arange(capacity) < block_live * GROUP)[:, None]
    q_rows = jnp.where(live_rows, query, 0.0)
    k_rows = jnp.where(live_rows, key_in, 0.0)
    v_rows = jnp.where(live_rows, value, 0.0)
    causal = jnp.tril(jnp.ones((GROUP, GROUP), dtype=bool))
    block_total = capacity // GROUP
    zero_state = jnp.zeros((features_dev, features_dev), jnp.float32)

    def forward_step(block_idx, state_pack):
        running, outputs, saved_states, saved_scores = state_pack
        row_start = block_idx * GROUP
        q_block = lax.dynamic_slice_in_dim(q_rows, row_start, GROUP, 0)
        k_block = lax.dynamic_slice_in_dim(k_rows, row_start, GROUP, 0)
        v_block = lax.dynamic_slice_in_dim(v_rows, row_start, GROUP, 0)
        scores = jnp.where(causal, plain_product(q_block, k_block.T), 0.0)
        local_part = plain_product(q_block, running) + plain_product(scores, v_block)
        outputs = lax.dynamic_update_slice_in_dim(outputs, local_part, row_start, 0)
        saved_states = lax.dynamic_update_index_in_dim(saved_states, running, block_idx, 0)
        saved_scores = lax.dynamic_update_index_in_dim(saved_scores, scores, block_idx, 0)
        running = running + leading_product(k_block, v_block)
        return (running, outputs, saved_states, saved_scores)

    forward_init = (
        zero_state,
        jnp.zeros((capacity, features_dev), jnp.float32),
        jnp.zeros((block_total, features_dev, features_dev), jnp.float32),
        jnp.zeros((block_total, GROUP, GROUP), jnp.float32),
    )
    shard_state, local_out, saved_states, saved_scores = lax.fori_loop(
        0, block_live, forward_step, forward_init
    )
    piece_rows = lax.all_gather(shard_state[None], "seq", axis=0, tiled=True)
    picked = (jnp.arange(piece_rows.shape[0]) < shard_pos)[:, None, None]
    state_in = jnp.sum(jnp.where(picked, piece_rows, 0.0), axis=0)
    attended = local_out + plain_product(q_rows, state_in)
    scaled = attended * head_scale[0]
    features = features_dev * lax.axis_size("head")
    squares, cross_terms = lax.psum(
        (jnp.sum(scaled * scaled, axis=1), jnp.sum(norm_gain[None, :] * out_grad * scaled, axis=1)),
        "head",
    )
    inverse = lax.rsqrt(squares / features + 1e-05)[:, None]
    normed = scaled * inverse * norm_gain[None, :]
    grad_scaled = (
        inverse * norm_gain[None, :] * out_grad
        - scaled * inverse * inverse * inverse * cross_terms[:, None] / features
    )
    grad_out = grad_scaled * head_scale[0]

    def backward_step(step_idx, state_pack):
        running, grad_q, grad_k, grad_v = state_pack
        block_idx = block_live - 1 - step_idx
        row_start = block_idx * GROUP
        q_block = lax.dynamic_slice_in_dim(q_rows, row_start, GROUP, 0)
        k_block = lax.dynamic_slice_in_dim(k_rows, row_start, GROUP, 0)
        v_block = lax.dynamic_slice_in_dim(v_rows, row_start, GROUP, 0)
        grad_block = lax.dynamic_slice_in_dim(grad_out, row_start, GROUP, 0)
        held_state = lax.dynamic_index_in_dim(saved_states, block_idx, 0, keepdims=False)
        scores = lax.dynamic_index_in_dim(saved_scores, block_idx, 0, keepdims=False)
        grad_vals = jnp.where(causal, plain_product(grad_block, v_block.T), 0.0)
        query_part = plain_product(grad_block, held_state.T) + plain_product(grad_vals, k_block)
        key_part = leading_product(grad_vals, q_block) + plain_product(v_block, running.T)
        value_part = leading_product(scores, grad_block) + plain_product(k_block, running)
        grad_q = lax.dynamic_update_slice_in_dim(grad_q, query_part, row_start, 0)
        grad_k = lax.dynamic_update_slice_in_dim(grad_k, key_part, row_start, 0)
        grad_v = lax.dynamic_update_slice_in_dim(grad_v, value_part, row_start, 0)
        running = running + leading_product(q_block, grad_block)
        return (running, grad_q, grad_k, grad_v)

    zero_rows = jnp.zeros((capacity, features_dev), jnp.float32)
    shard_grad, grad_q, grad_k, grad_v = lax.fori_loop(
        0, block_live, backward_step, (zero_state, zero_rows, zero_rows, zero_rows)
    )
    piece_rows = lax.all_gather(shard_grad[None], "seq", axis=0, tiled=True)
    picked = (jnp.arange(piece_rows.shape[0]) > shard_pos)[:, None, None]
    state_out = jnp.sum(jnp.where(picked, piece_rows, 0.0), axis=0)
    grad_query = jnp.where(live_rows, grad_q + plain_product(grad_out, state_in.T), 0.0)
    grad_key = jnp.where(live_rows, grad_k + plain_product(v_rows, state_out.T), 0.0)
    grad_value = jnp.where(live_rows, grad_v + plain_product(k_rows, state_out), 0.0)
    return (normed, grad_query, grad_key, grad_value)


def solution(mesh):
    in_specs = (
        P("seq", "head"),
        P("seq", "head"),
        P("seq", "head"),
        P("seq", "head"),
        P("head"),
        P("head"),
        P(),
    )
    out_specs = (P("seq", "head"), P("seq", "head"), P("seq", "head"), P("seq", "head"))
    return jax.shard_map(
        on_device, mesh=mesh, in_specs=in_specs, out_specs=out_specs, check_vma=False
    )
```

profile of v0, /device:TPU:0, one launch (start us, length us, event | category | flops | bytes accessed | tf_op | source)
XLA Modules:
  0.0 91.5 jit_solution(258238342465137067)
XLA Ops:
  0.6 0.0 copy-start.1
  0.7 1.2 %copy.12 = f32[768,128]{0,1:T(8,128)S(1)} copy(f32[768,128]{1,0:T(8,128)} %param.14) | data formatting | bytes 786432 | tf_op args[3]
  2.5 0.0 copy-start.6
  2.6 0.6 copy-done.6
  3.2 0.7 dynamic_slice.43
  4.6 1.2 %broadcast_select_fusion = (f32[768,128]{1,0:T(8,128)S(1)}, f32[768,128]{1,0:T(8,128)S(1)}, f32[768,128]{1,0:T(8,128)S(1)}) fusion(f32[768,128]{1,0:T(8,128)} %param.11, pred[768]{0:T(1024)(128)(4,1)S(1)} %iota_compare_fusion.2, f32[768,128]{1,0:T(8,128)S(1)} %copy-done, f32[768,128]{1,0:T(8,128)S(1)} %copy-done.1), kind=kLoop, calls=%fused_computation.68 | loop fusion | flops 294912 | bytes 2360064 | tf_op jit(solution)/shard_map/jit(_where)/select_n | solution.py:28
  5.9 4.4 %while.36 = (s32[]{:T(128)}, f32[128,128]{1,0:T(8,128)S(1)}, f32[768,128]{0,1:T(8,128)S(1)}, f32[6,128,128]{2,1,0:T(8,128)S(1)}, f32[6,128,128]{2,1,0:T(8,128)S(...) while((s32[]{:T(128)}, f32[128,128]{1,0:T(8,128)S(1)}, ...), condition=%wide.region_1.2_spmd.clone, body=%wide.region_0.1_spmd.clone.sunk | while | flops 100728832 | bytes 1379053 | solution.py:55
  6.6 0.2 fusion.94
  6.8 0.3 convolution_add_fusion.13
  7.1 0.3 bitcast_dynamic-update-slice_fusion.4
  7.4 0.2 convolution_add_fusion.14
  7.6 0.1 copy.24
  8.5 0.2 fusion.94
  8.7 0.3 convolution_add_fusion.13
  9.0 0.3 bitcast_dynamic-update-slice_fusion.4
  9.3 0.2 convolution_add_fusion.14
  9.5 0.1 copy.24
  10.3 0.0 copy-start.3
  10.3 0.0 copy-start.4
  10.3 20.9 %all-gather = f32[512,128]{1,0:T(8,128)S(1)} all-gather(f32[128,128]{1,0:T(8,128)S(1)} %get-tuple-element.221), channel_id=2, replica_groups=mesh['seq'=4,'head'=8] {'seq'}, dimensions={0}, use_global_device_ids=true | all-gather | bytes 327680 | tf_op jit(solution)/shard_map/all_gather | solution.py:58
  31.2 0.1 select_reduce_fusion.1
  31.3 0.6 copy-done.5
  31.9 0.6 multiply_reduce_fusion
  32.5 12.1 %all-reduce = (f32[768]{0:T(1024)S(1)}, f32[768]{0:T(1024)S(1)}) all-reduce(f32[768]{0:T(1024)S(1)} %get-tuple-element.296, f32[768]{0:T(1024)S(1)} %get-tuple-element.295), channel_id=1, replica_groups=mesh['seq'=4,'head'=8] {'head'}, use_global_device_ids=true, to_apply=%region_4.5 | all-reduce | flops 1536 | bytes 12288 | tf_op jit(solution)/shard_map/psum | solution.py:64
  44.6 0.1 subtract_multiply_fusion
  44.8 0.9 copy.15
  46.5 9.9 %while.37 = (s32[]{:T(128)}, f32[128,128]{1,0:T(8,128)S(1)}, f32[768,128]{1,0:T(8,128)S(1)}, f32[768,128]{1,0:T(8,128)S(1)}, f32[768,128]{1,0:T(8,128)S(1)}, /*i...) while((s32[]{:T(128)}, f32[128,128]{1,0:T(8,128)S(1)}, ...), condition=%wide.region_8.9_spmd.clone, body=%wide.region_7.8_spmd.clone.sunk | while | flops 201424896 | bytes 1840413 | solution.py:97
  47.2 1.1 %fusion.115 = f32[128,128]{1,0:T(8,128)S(1)} fusion(f32[6,128,128]{2,1,0:T(8,128)} %get-tuple-element.581, s32[]{:T(128)S(6)} %select_n.105, f32[768,128]{0,1:T(8,128)S(1)} %get-tuple-element.577, s32[]{:T(128)S(6)} %select_n.104), kind=kOutput, calls=%fused_computation.28.clone.1 | convolution fusion | flops 25165824 | bytes 196616 | tf_op jit(solution)/shard_map/while/body/dot_general | solution.py:14
  48.3 0.2 fusion.116
  48.6 0.3 convolution_select_fusion.3
  48.9 0.3 fusion.113
  49.2 0.3 fusion.114
  49.4 0.3 convolution_add_fusion.15
  49.7 1.1 %fusion.111 = f32[128,128]{1,0:T(8,128)S(1)} fusion(f32[6,128,128]{2,1,0:T(8,128)} %get-tuple-element.578, s32[]{:T(128)S(6)} %select_n.105, f32[768,128]{0,1:T(8,128)S(1)} %get-tuple-element.577, s32[]{:T(128)S(6)} %select_n.104), kind=kOutput, calls=%fused_computation.30.clone.1 | convolution fusion | flops 25165824 | bytes 196616 | tf_op jit(solution)/shard_map/while/body/dot_general | solution.py:10
  50.9 0.2 fusion.112
  51.8 1.1 %fusion.115 = f32[128,128]{1,0:T(8,128)S(1)} fusion(f32[6,128,128]{2,1,0:T(8,128)} %get-tuple-element.581, s32[]{:T(128)S(6)} %select_n.105, f32[768,128]{0,1:T(8,128)S(1)} %get-tuple-element.577, s32[]{:T(128)S(6)} %select_n.104), kind=kOutput, calls=%fused_computation.28.clone.1 | convolution fusion | flops 25165824 | bytes 196616 | tf_op jit(solution)/shard_map/while/body/dot_general | solution.py:14
  52.9 0.2 fusion.116
  53.2 0.3 convolution_select_fusion.3
  53.5 0.3 fusion.113
  53.8 0.3 fusion.114
  54.0 0.3 convolution_add_fusion.15
  54.3 1.1 %fusion.111 = f32[128,128]{1,0:T(8,128)S(1)} fusion(f32[6,128,128]{2,1,0:T(8,128)} %get-tuple-element.578, s32[]{:T(128)S(6)} %select_n.105, f32[768,128]{0,1:T(8,128)S(1)} %get-tuple-element.577, s32[]{:T(128)S(6)} %select_n.104), kind=kOutput, calls=%fused_computation.30.clone.1 | convolution fusion | flops 25165824 | bytes 196616 | tf_op jit(solution)/shard_map/while/body/dot_general | solution.py:10
  55.5 0.2 fusion.112
  56.4 1.5 %fusion.44 = f32[768,128]{1,0:T(8,128)} fusion(f32[768,128]{1,0:T(8,128)S(1)} %get-tuple-element.224, f32[768,128]{0,1:T(8,128)S(1)} %get-tuple-element.587, f32[128,128]{1,0:T(8,128)S(1)} %select_reduce_fusion.1, pred[768]{0:T(1024)(128)(4,1)S(1)} %iota_compare_fusion.2), kind=kOutput, calls=%fused_computation.59 | convolution fusion | flops 151191552 | bytes 1245952 | tf_op jit(solution)/shard_map/dot_general | solution.py:10
  57.9 30.9 %all-gather.1 = f32[512,128]{1,0:T(8,128)S(1)} all-gather(f32[128,128]{1,0:T(8,128)S(1)} %get-tuple-element.226), channel_id=3, replica_groups=mesh['seq'=4,'head'=8] {'seq'}, dimensions={0}, use_global_device_ids=true | all-gather | bytes 327680 | tf_op jit(solution)/shard_map/all_gather | solution.py:100
  88.8 0.1 select_reduce_fusion
  88.9 1.3 %fusion.45 = f32[768,128]{1,0:T(8,128)} fusion(f32[768,128]{1,0:T(8,128)S(1)} %get-tuple-element.225, f32[128,128]{1,0:T(8,128)S(1)} %select_reduce_fusion, pred[768]{0:T(1024)(128)(4,1)S(1)} %iota_compare_fusion.2, f32[768,128]{1,0:T(8,128)S(1)} %copy-done), kind=kOutput, calls=%fused_computation.60 | convolution fusion | flops 151289856 | bytes 1245952 | tf_op jit(solution)/shard_map/dot_general | solution.py:10
  90.2 1.3 %fusion.46 = f32[768,128]{1,0:T(8,128)} fusion(f32[768,128]{1,0:T(8,128)S(1)} %get-tuple-element.227, f32[128,128]{1,0:T(8,128)S(1)} %select_reduce_fusion, pred[768]{0:T(1024)(128)(4,1)S(1)} %iota_compare_fusion.2, f32[768,128]{1,0:T(8,128)S(1)} %copy-done.2), kind=kOutput, calls=%fused_computation.61 | convolution fusion | flops 151289856 | bytes 1245952 | tf_op jit(solution)/shard_map/dot_general | solution.py:10
  (24 shorter events, 0.3 us)
Async XLA Ops:
  0.6 3.9 %copy-start = (f32[768,128]{1,0:T(8,128)S(1)}, f32[768,128]{1,0:T(8,128)}, u32[]{:S(2)}) copy-start(f32[768,128]{1,0:T(8,128)} %param.13) | copy-start | bytes 1179652
  0.6 3.9 %copy-start.1 = (f32[768,128]{1,0:T(8,128)S(1)}, f32[768,128]{1,0:T(8,128)}, u32[]{:S(2)}) copy-start(f32[768,128]{1,0:T(8,128)} %param.12) | copy-start | bytes 1179652
  2.5 0.7 copy-start.6
  10.3 20.9 %copy-start.3 = (f32[6,128,128]{2,1,0:T(8,128)}, f32[6,128,128]{2,1,0:T(8,128)S(1)}, u32[]{:S(2)}) copy-start(f32[6,128,128]{2,1,0:T(8,128)S(1)} %get-tuple-element.542) | copy-start | bytes 1179652
  10.3 22.1 %copy-start.4 = (f32[6,128,128]{2,1,0:T(8,128)}, f32[6,128,128]{2,1,0:T(8,128)S(1)}, u32[]{:S(2)}) copy-start(f32[6,128,128]{2,1,0:T(8,128)S(1)} %get-tuple-element.545) | copy-start | bytes 1179652
  31.2 0.7 copy-start.5
  88.9 1.3 %copy-start.2 = (f32[768,128]{1,0:T(8,128)S(1)}, f32[768,128]{1,0:T(8,128)}, u32[]{:S(2)}) copy-start(f32[768,128]{1,0:T(8,128)} %param.12) | copy-start | bytes 1179652
where the time goes:
time: 92.4 us; the launch traced here: 91.5 us
  blocking collectives  63.9 us (69%)
  matrix products  14.3 us (15%)
  loops' own time  4.45 us (5%)
  local copies, waits for them, and re-layouts  4.44 us (5%)
  between operations  2.89 us (3%)
  other arithmetic  1.52 us (2%)
    all_gather x1, blocking collectives, on_device(): piece_rows = lax.all_gather(shard_grad[None], 'seq', axis=0, tiled=True)  30.9 us
    all_gather x1, blocking collectives, on_device(): piece_rows = lax.all_gather(shard_state[None], 'seq', axis=0, tiled=True)  20.9 us
    psum x1, blocking collectives, on_device(): lax.psum((jnp.sum(scaled * scaled, axis=1), jnp.sum(norm_gain[None, :] *...  12.1 us
    dot_general x20, matrix products, plain_product(): jnp.dot(left, right, precision=lax.Precision.HIGHEST, preferred_element_t...  10.3 us
    dot_general x8, matrix products, leading_product(): lax.dot_general(left, right, (((0,), (0,)), ((), ())), precision=lax.Prec...  4 us
    unnamed x16, local copies, waits for them, and re-layouts  3.38 us
    another operation x1, loops' own time, on_device(): lax.fori_loop(0, block_live, backward_step, (zero_state, zero_rows, zero_...  2.23 us
    another operation x1, loops' own time, on_device(): lax.fori_loop(0, block_live, forward_step, forward_init)  2.22 us

commit v1 on v0

--- a/solution.py
+++ b/solution.py
@@ -4,6 +4,24 @@
 from jax.sharding import PartitionSpec as P
 
 GROUP = 128
+
+
+def in_order(blocks, dim):
+    blocks = jnp.moveaxis(blocks, 0, dim)
+    lengths = blocks.shape
+    return blocks.reshape(*lengths[:dim], lengths[dim] * lengths[dim + 1], *lengths[dim + 2 :])
+
+
+def doubled(x, axis):
+    size = lax.axis_size(axis)
+    blocks = x[None]
+    for level in range(size.bit_length() - 1):
+        apart = 1 << level
+        other = lax.ppermute(blocks, axis, [(i, i ^ apart) for i in range(size)])
+        both = jnp.stack([blocks, other])
+        upper = lax.axis_index(axis) >> level & 1
+        blocks = jnp.where(upper == 0, both, both[::-1]).reshape(-1, *x.shape)
+    return blocks
 
 
 def plain_product(left, right):
@@ -55,7 +73,7 @@
     shard_state, local_out, saved_states, saved_scores = lax.fori_loop(
         0, block_live, forward_step, forward_init
     )
-    piece_rows = lax.all_gather(shard_state[None], "seq", axis=0, tiled=True)
+    piece_rows = in_order(doubled(shard_state[None], "seq"), 0)
     picked = (jnp.arange(piece_rows.shape[0]) < shard_pos)[:, None, None]
     state_in = jnp.sum(jnp.where(picked, piece_rows, 0.0), axis=0)
     attended = local_out + plain_product(q_rows, state_in)

time: 92.4 us -> 82 us (0.89)
  blocking collectives: 63.9 us -> 37.4 us
  starting transfers between devices: 0 us -> 10.4 us
  waiting for transfers between devices: 0 us -> 8.79 us
  matrix products: 14.3 us -> 12.6 us
  local copies, waits for them, and re-layouts: 4.44 us -> 3.37 us
    all_gather x1 -> x0, blocking collectives: 20.9 us -> none  [on_device(): piece_rows = lax.all_gather(shard_state[None], 'seq', axis=0, tiled=True)]
    ppermute x0 -> x2, starting transfers between devices: none -> 10.4 us  [doubled(): other = lax.ppermute(blocks, axis, [(i, i ^ apart) for i in range(size)])]
    ppermute x0 -> x2, waiting for transfers between devices: none -> 8.79 us  [doubled(): other = lax.ppermute(blocks, axis, [(i, i ^ apart) for i in range(size)])]
    all_gather x1, blocking collectives: 30.9 us -> 25.3 us  [on_device(): piece_rows = lax.all_gather(shard_grad[None], 'seq', axis=0, tiled=True)]
    dot_general x20, matrix products: 10.3 us -> 8.62 us  [plain_product(): jnp.dot(left, right, precision=lax.Precision.HIGHEST, preferred_element_t...]
    unnamed x16 -> x14, local copies, waits for them, and re-layouts: 3.38 us -> 2.4 us
  transfers between devices with their start and end apart: 0 -> 2, of which waited for: 0 -> 2; matrix products, arithmetic and copies ran while one was open for 0% -> 0% of each run, Pallas kernels for 0% -> 0%
where the time goes in v1:
time: 82 us; the launch traced here: 81.4 us
  blocking collectives  37.4 us (46%)
  matrix products  12.6 us (15%)
  starting transfers between devices  10.4 us (13%)
  waiting for transfers between devices  8.79 us (11%)
  loops' own time  4.19 us (5%)
  local copies, waits for them, and re-layouts  3.37 us (4%)
  between operations  2.81 us (3%)
  other arithmetic  1.81 us (2%)
    all_gather x1, blocking collectives, on_device(): piece_rows = lax.all_gather(shard_grad[None], 'seq', axis=0, tiled=True)  25.3 us
    psum x1, blocking collectives, on_device(): lax.psum((jnp.sum(scaled * scaled, axis=1), jnp.sum(norm_gain[None, :] *...  12.1 us
    ppermute x2, starting transfers between devices, doubled(): other = lax.ppermute(blocks, axis, [(i, i ^ apart) for i in range(size)])  10.4 us
    ppermute x2, waiting for transfers between devices, doubled(): other = lax.ppermute(blocks, axis, [(i, i ^ apart) for i in range(size)])  8.79 us
    dot_general x20, matrix products, plain_product(): jnp.dot(left, right, precision=lax.Precision.HIGHEST, preferred_element_t...  8.62 us
    dot_general x8, matrix products, leading_product(): lax.dot_general(left, right, (((0,), (0,)), ((), ())), precision=lax.Prec...  4 us
    unnamed x14, local copies, waits for them, and re-layouts  2.4 us
    another operation x1, loops' own time, on_device(): lax.fori_loop(0, block_live, backward_step, (zero_state, zero_rows, zero_...  2.11 us
  transfers between devices with their start and end apart: 2, of which 2 were waited for; matrix products, arithmetic and copies ran while one was open for 0% of the time, Pallas kernels for 0%

profile of v1, /device:TPU:0, one launch (start us, length us, event | category | flops | bytes accessed | tf_op | source)
XLA Modules:
  0.0 81.4 jit_solution(16147412140604203455)
XLA Ops:
  0.6 0.6 copy-done.5
  1.3 0.6 dynamic_slice.43
  2.5 1.4 %broadcast_select_fusion = (f32[768,128]{1,0:T(8,128)S(1)}, f32[768,128]{1,0:T(8,128)S(1)}, f32[768,128]{1,0:T(8,128)S(1)}) fusion(f32[768,128]{1,0:T(8,128)} %param.11, pred[768]{0:T(1024)(128)(4,1)S(1)} %iota_compare_fusion.2, f32[768,128]{1,0:T(8,128)} %param.13, f32[768,128]{1,0:T(8,128)} %param.12), kind=kLoop, calls=%fused_computation.72 | loop fusion | flops 294912 | bytes 2360064 | tf_op jit(solution)/shard_map/jit(_where)/select_n | solution.py:46
  4.1 4.3 %while.36 = (s32[]{:T(128)}, f32[128,128]{1,0:T(8,128)S(1)}, f32[768,128]{0,1:T(8,128)S(1)}, f32[6,128,128]{2,1,0:T(8,128)S(1)}, f32[6,128,128]{2,1,0:T(8,128)S(...) while((s32[]{:T(128)}, f32[128,128]{1,0:T(8,128)S(1)}, ...), condition=%wide.region_1.2_spmd.clone, body=%wide.region_0.1_spmd.clone.sunk | while | flops 100728832 | bytes 1379053 | solution.py:73
  4.8 0.2 fusion.98
  5.0 0.3 convolution_add_fusion.13
  5.3 0.3 bitcast_dynamic-update-slice_fusion.4
  5.5 0.2 convolution_add_fusion.14
  5.8 0.1 copy.24
  6.6 0.2 fusion.98
  6.8 0.3 convolution_add_fusion.13
  7.1 0.3 bitcast_dynamic-update-slice_fusion.4
  7.4 0.2 convolution_add_fusion.14
  7.6 0.1 copy.24
  8.4 0.0 copy-start.2
  8.4 10.4 %collective-permute-start = (f32[1,1,128,128]{3,2,1,0:T(8,128)S(1)}, f32[1,1,128,128]{3,2,1,0:T(8,128)S(1)}, u32[]{:S(2)}, u32[]{:S(2)}) collective-permute-start(f32[1,1,128,128]{3,2,1,0:T(8,128)S(1)} %bitcast.55), channel_id=1, source_target_pairs={{0,8},{8,0},{16,24},{24,16},{1,9},{9,1},{17,25},{25,17},{2,10},{10... | collective-permute-start | bytes 196616 | tf_op jit(solution)/shard_map/ppermute | solution.py:20
  18.7 2.2 %collective-permute-done = f32[1,1,128,128]{3,2,1,0:T(8,128)S(1)} collective-permute-done((f32[1,1,128,128]{3,2,1,0:T(8,128)S(1)}, f32[1,1,128,128]{3,2,1,0:T(8,128)S(1)}, u32[]{:S(2)}, u32[]{:S(2)}) %collective-permute-start) | collective-permute-done | bytes 65568 | tf_op jit(solution)/shard_map/ppermute | solution.py:20
  21.0 0.1 collective-permute-start.1
  21.1 0.2 copy.12
  22.6 6.5 %collective-permute-done.1 = f32[2,1,128,128]{3,2,0,1:T(8,128)S(1)} collective-permute-done((f32[2,1,128,128]{3,2,0,1:T(8,128)S(1)}, f32[2,1,128,128]{3,2,0,1:T(8,128)S(1)}, u32[]{:S(2)}, u32[]{:S(2)}) %collective-permute-start.1) | collective-permute-done | bytes 131104 | tf_op jit(solution)/shard_map/ppermute | solution.py:20
  29.2 0.1 fusion.48
  29.3 0.6 copy-done.4
  30.0 0.6 multiply_reduce_fusion
  30.5 12.1 %all-reduce = (f32[768]{0:T(1024)S(1)}, f32[768]{0:T(1024)S(1)}) all-reduce(f32[768]{0:T(1024)S(1)} %get-tuple-element.296, f32[768]{0:T(1024)S(1)} %get-tuple-element.295), channel_id=1, replica_groups=mesh['seq'=4,'head'=8] {'head'}, use_global_device_ids=true, to_apply=%region_4.5 | all-reduce | flops 1536 | bytes 12288 | tf_op jit(solution)/shard_map/psum | solution.py:82
  42.7 0.1 subtract_multiply_fusion
  42.8 0.9 %copy.15 = f32[768,128]{1,0:T(8,128)} copy(f32[768,128]{0,1:T(8,128)S(1)} %get-tuple-element.346) | data formatting | bytes 786432
  43.9 8.1 %while.37 = (s32[]{:T(128)}, f32[128,128]{1,0:T(8,128)S(1)}, f32[768,128]{1,0:T(8,128)S(1)}, f32[768,128]{1,0:T(8,128)S(1)}, f32[768,128]{1,0:T(8,128)S(1)}, /*i...) while((s32[]{:T(128)}, f32[128,128]{1,0:T(8,128)S(1)}, ...), condition=%wide.region_8.9_spmd.clone, body=%wide.region_7.8_spmd.clone.sunk | while | flops 201424896 | bytes 1840413 | solution.py:115
  44.5 1.1 %fusion.119 = f32[128,128]{1,0:T(8,128)S(1)} fusion(f32[6,128,128]{2,1,0:T(8,128)} %get-tuple-element.583, s32[]{:T(128)S(6)} %select_n.141, f32[768,128]{0,1:T(8,128)S(1)} %get-tuple-element.579, s32[]{:T(128)S(6)} %select_n.140), kind=kOutput, calls=%fused_computation.28.clone.1 | convolution fusion | flops 25165824 | bytes 196616 | tf_op jit(solution)/shard_map/while/body/dot_general | solution.py:32
  45.7 0.2 fusion.120
  45.9 0.3 convolution_select_fusion.3
  46.2 0.3 fusion.117
  46.5 0.3 fusion.118
  46.8 0.3 convolution_add_fusion.15
  47.1 0.3 fusion.115
  47.4 0.2 fusion.116
  48.2 1.1 %fusion.119 = f32[128,128]{1,0:T(8,128)S(1)} fusion(f32[6,128,128]{2,1,0:T(8,128)} %get-tuple-element.583, s32[]{:T(128)S(6)} %select_n.141, f32[768,128]{0,1:T(8,128)S(1)} %get-tuple-element.579, s32[]{:T(128)S(6)} %select_n.140), kind=kOutput, calls=%fused_computation.28.clone.1 | convolution fusion | flops 25165824 | bytes 196616 | tf_op jit(solution)/shard_map/while/body/dot_general | solution.py:32
  49.4 0.2 fusion.120
  49.6 0.3 convolution_select_fusion.3
  49.9 0.3 fusion.117
  50.2 0.3 fusion.118
  50.5 0.3 convolution_add_fusion.15
  50.8 0.3 fusion.115
  51.1 0.2 fusion.116
  51.9 1.5 %fusion.44 = f32[768,128]{1,0:T(8,128)} fusion(f32[768,128]{1,0:T(8,128)S(1)} %get-tuple-element.224, f32[768,128]{0,1:T(8,128)S(1)} %get-tuple-element.590, f32[128,128]{1,0:T(8,128)S(1)} %fusion.48, pred[768]{0:T(1024)(128)(4,1)S(1)} %iota_compare_fusion.2), kind=kOutput, calls=%fused_computation.59 | convolution fusion | flops 151191552 | bytes 1245952 | tf_op jit(solution)/shard_map/dot_general | solution.py:28
  53.5 25.3 %all-gather = f32[512,128]{1,0:T(8,128)S(1)} all-gather(f32[128,128]{1,0:T(8,128)S(1)} %get-tuple-element.226), channel_id=2, replica_groups=mesh['seq'=4,'head'=8] {'seq'}, dimensions={0}, use_global_device_ids=true | all-gather | bytes 327680 | tf_op jit(solution)/shard_map/all_gather | solution.py:118
  78.7 0.1 select_reduce_fusion
  78.9 1.3 %fusion.45 = f32[768,128]{1,0:T(8,128)} fusion(f32[768,128]{1,0:T(8,128)S(1)} %get-tuple-element.225, f32[128,128]{1,0:T(8,128)S(1)} %select_reduce_fusion, pred[768]{0:T(1024)(128)(4,1)S(1)} %iota_compare_fusion.2, f32[768,128]{1,0:T(8,128)S(1)} %copy-done), kind=kOutput, calls=%fused_computation.60 | convolution fusion | flops 151289856 | bytes 1245952 | tf_op jit(solution)/shard_map/dot_general | solution.py:28
  80.1 1.3 %fusion.46 = f32[768,128]{1,0:T(8,128)} fusion(f32[768,128]{1,0:T(8,128)S(1)} %get-tuple-element.227, f32[128,128]{1,0:T(8,128)S(1)} %select_reduce_fusion, pred[768]{0:T(1024)(128)(4,1)S(1)} %iota_compare_fusion.2, f32[768,128]{1,0:T(8,128)S(1)} %copy-done.1), kind=kOutput, calls=%fused_computation.61 | convolution fusion | flops 151289856 | bytes 1245952 | tf_op jit(solution)/shard_map/dot_general | solution.py:28
  (28 shorter events, 0.3 us)
Async XLA Ops:
  0.6 0.7 copy-start.5
  8.4 12.8 %copy-start.2 = (f32[6,128,128]{2,1,0:T(8,128)}, f32[6,128,128]{2,1,0:T(8,128)S(1)}, u32[]{:S(2)}) copy-start(f32[6,128,128]{2,1,0:T(8,128)S(1)} %get-tuple-element.547) | copy-start | bytes 1179652
  8.4 12.8 %copy-start.3 = (f32[768,128]{1,0:T(8,128)S(1)}, f32[768,128]{1,0:T(8,128)}, u32[]{:S(2)}) copy-start(f32[768,128]{1,0:T(8,128)} %param.14) | copy-start | bytes 1179652
  8.4 12.6 %collective-permute-start = (f32[1,1,128,128]{3,2,1,0:T(8,128)S(1)}, f32[1,1,128,128]{3,2,1,0:T(8,128)S(1)}, u32[]{:S(2)}, u32[]{:S(2)}) collective-permute-start(f32[1,1,128,128]{3,2,1,0:T(8,128)S(1)} %bitcast.55), channel_id=1, source_target_pairs={{0,8},{8,0},{16,24},{24,16},{1,9},{9,1},{17,25},{25,17},{2,10},{10... | collective-permute-start | bytes 196616 | tf_op jit(solution)/shard_map/ppermute | solution.py:20
  21.0 8.1 %collective-permute-start.1 = (f32[2,1,128,128]{3,2,0,1:T(8,128)S(1)}, f32[2,1,128,128]{3,2,0,1:T(8,128)S(1)}, u32[]{:S(2)}, u32[]{:S(2)}) collective-permute-start(f32[2,1,128,128]{3,2,0,1:T(8,128)S(1)} %get-tuple-element.348), channel_id=1, source_target_pairs={{0,16},{8,24},{16,0},{24,8},{1,17},{9,25},{17,1},{25,9},{2,18},{10... | collective-permute-start | bytes 393224 | tf_op jit(solution)/shard_map/ppermute | solution.py:20
  29.3 0.7 copy-start.4
  53.5 25.4 %copy-start = (f32[768,128]{1,0:T(8,128)S(1)}, f32[768,128]{1,0:T(8,128)}, u32[]{:S(2)}) copy-start(f32[768,128]{1,0:T(8,128)} %param.13) | copy-start | bytes 1179652
  78.8 1.3 %copy-start.1 = (f32[768,128]{1,0:T(8,128)S(1)}, f32[768,128]{1,0:T(8,128)}, u32[]{:S(2)}) copy-start(f32[768,128]{1,0:T(8,128)} %param.12) | copy-start | bytes 1179652
